TPU v7x, 32 devices: a whole 2x2x4 slice. The times are simulated.
32 devices in a mesh: dp: 8 (over z, x), tensor: 4 (over y, core).
Axes of the slice: x: 2, y: 2, z: 4, core: 2. Of those that a mesh axis runs over, the one named last changes fastest.
Arguments:
- tokens: bfloat16 [32768, 1024], P('dp', 'tensor'), may hold values from -6 to 6
- lengths: int32 [16], P('dp'), may hold values from 512 to 2048, as said below
- grad_out: bfloat16 [32768, 1024], P('dp', 'tensor'), may hold values from -6 to 6
- norm_gain: bfloat16 [1024], P('dp'), may hold values from 0.099609375 to 1.8984375
- w_gate: bfloat16 [1024, 2048], P('dp', 'tensor'), may hold values from -0.1875 to 0.1875
- w_value: bfloat16 [1024, 2048], P('dp', 'tensor'), may hold values from -0.1875 to 0.1875
- w_bc: bfloat16 [1024, 256], P('dp'), may hold values from -0.1875 to 0.1875
- w_dt: bfloat16 [1024, 32], P('dp', 'tensor'), may hold values from -0.1875 to 0.1875
- conv_x: float32 [5, 2048], P(None, 'tensor'), may hold values from -3 to 3
- conv_bc: float32 [5, 256], replicated, may hold values from -3 to 3
- dt_bias: float32 [32], P('tensor'), may hold values from -7 to -2.5
- a_log: float32 [32], P('tensor'), may hold values from 0 to 2.77
- skip_d: float32 [32], P('tensor'), may hold values from 0.35 to 2.75
- gate_gain: float32 [2048], P('tensor'), may hold values from 0.1 to 1.9
- w_out: bfloat16 [1024, 2048], P('dp', 'tensor'), may hold values from -0.125 to 0.125
Outputs:
- out: bfloat16 [32768, 1024], P('dp', 'tensor')
- grad_tokens: float32 [32768, 1024], P('dp', 'tensor')
- grad_norm_gain: float32 [1024], P(('dp', 'tensor'))
- grad_w_gate: float32 [1024, 2048], P('dp', 'tensor')
- grad_w_value: float32 [1024, 2048], P('dp', 'tensor')
- grad_w_bc: float32 [1024, 256], P(('dp', 'tensor'))
- grad_w_dt: float32 [1024, 32], P('dp', 'tensor')
- grad_conv_x: float32 [5, 2048], P(None, 'tensor')
- grad_conv_bc: float32 [5, 256], replicated
- grad_dt_bias: float32 [32], P('tensor')
- grad_a_log: float32 [32], P('tensor')
- grad_skip_d: float32 [32], P('tensor')
- grad_gate_gain: float32 [2048], P('tensor')
- grad_w_out: float32 [1024, 2048], P('dp', 'tensor')
Inputs may be any that keep to these rules, and one draw needn't show every extreme that they name: Sequence i occupies the first lengths[i] of its 2048 slots; the rest is padding. Sequence 0 is full.
All inputs are finite; a program needn't handle non-finite values.
Results may differ from a plain program's by a relative error of at most 0.0085.
Values may be sent and summed in bfloat16 or wider, within the bound.
No kernel may reach another device: no remote copies, remote signals or barrier semaphores. Data moves between devices by JAX's collectives and lax.ppermute only.
A program may use at most 192 MiB of HBM per device.

v0:
```python
import jax
import jax.numpy as jnp
from jax import lax
from jax.sharding import PartitionSpec as P

GROUP = 256
SEQ_LEN = 2048
epsilon = 1e-05


def causal_conv(signal, kernel):
    window = kernel.shape[0] - 1
    length = signal.shape[0]
    padded = jnp.concatenate([jnp.zeros((window - 1, signal.shape[1]), jnp.float32), signal], 0)
    summed = jnp.broadcast_to(kernel[window], signal.shape)
    for offset in range(window):
        summed = summed + kernel[offset] * padded[offset : offset + length]
    return summed


def group_scan(values, step_sizes, decay_rates, inputs_b, inputs_c):
    length, head_count, head_width = values.shape
    blocks = length // GROUP
    values = values.reshape(blocks, GROUP, head_count, head_width)
    step_sizes = step_sizes.reshape(blocks, GROUP, head_count)
    inputs_b = inputs_b.reshape(blocks, GROUP, -1)
    inputs_c = inputs_c.reshape(blocks, GROUP, -1)
    log_decay = jnp.transpose(step_sizes * decay_rates, (0, 2, 1))
    running = jnp.cumsum(log_decay, axis=2)
    causal = jnp.arange(GROUP)[:, None] >= jnp.arange(GROUP)[None, :]
    decay_grid = jnp.exp(jnp.where(causal, running[..., :, None] - running[..., None, :], -jnp.inf))
    intersection = jnp.einsum("bqn,bsn->bqs", inputs_c, inputs_b, precision=lax.Precision.HIGHEST)
    weighted = values * step_sizes[..., None]
    inner_part = jnp.einsum(
        "bhqs,bshp->bqhp",
        intersection[:, None] * decay_grid,
        weighted,
        precision=lax.Precision.HIGHEST,
    )
    to_end = jnp.exp(running[..., -1:] - running)
    states = jnp.einsum(
        "bsn,bhs,bshp->bhpn", inputs_b, to_end, weighted, precision=lax.Precision.HIGHEST
    )
    totals = running[..., -1]
    through = jnp.cumsum(totals, axis=0)
    before = through - totals
    earlier = jnp.arange(blocks)[:, None] > jnp.arange(blocks)[None, :]
    carry_weights = jnp.exp(
        jnp.where(earlier[..., None], before[:, None, :] - through[None, :, :], -jnp.inf)
    )
    incoming = jnp.einsum("cdh,dhpn->chpn", carry_weights, states, precision=lax.Precision.HIGHEST)
    outer_part = jnp.einsum(
        "bqn,bhpn,bhq->bqhp", inputs_c, incoming, jnp.exp(running), precision=lax.Precision.HIGHEST
    )
    return (inner_part + outer_part).reshape(length, head_count, head_width)


def mixer(
    gate_in, value_in, shared_in, step_in, conv_value, conv_shared, step_bias, log_rate, skip_gain
):
    length = value_in.shape[0]
    head_count = step_in.shape[1]
    state_size = shared_in.shape[1] // 2
    convolved = jax.nn.silu(causal_conv(value_in, conv_value))
    shared = jax.nn.silu(causal_conv(shared_in, conv_shared))
    step_sizes = jax.nn.softplus(step_in + step_bias)
    decay_rates = -jnp.exp(log_rate)
    values = convolved.reshape(length, head_count, -1)
    scanned = group_scan(
        values, step_sizes, decay_rates, shared[:, :state_size], shared[:, state_size:]
    )
    mixed_out = scanned + skip_gain[:, None] * values
    return mixed_out.reshape(length, -1) * jax.nn.silu(gate_in)


def over_rows(left, right):
    return lax.dot_general(
        left, right, (((0,), (0,)), ((), ())), preferred_element_type=jnp.float32
    )


def against(left, right):
    return lax.dot_general(
        left, right, (((1,), (1,)), ((), ())), preferred_element_type=jnp.float32
    )


def per_device(
    tokens,
    lengths,
    grad_out,
    norm_gain,
    w_gate,
    w_value,
    w_bc,
    w_dt,
    conv_x,
    conv_bc,
    dt_bias,
    a_log,
    skip_d,
    gate_gain,
    w_out,
):
    tensor_count = lax.axis_size("tensor")
    row_count, local_width = tokens.shape
    width_all = local_width * tensor_count
    inner_local = w_gate.shape[1]
    inner_all = inner_local * tensor_count
    micro_count = row_count // SEQ_LEN

    def micro_step(micro_index, carry):
        (
            out_rows,
            grad_rows,
            acc_gate,
            acc_value,
            acc_shared,
            acc_step,
            acc_out,
            acc_norm,
            acc_conv_value,
            acc_conv_shared,
            acc_bias,
            acc_rate,
            acc_skip,
            acc_gain,
        ) = carry
        start = micro_index * SEQ_LEN
        local_rows = lax.dynamic_slice_in_dim(tokens, start, SEQ_LEN, 0)
        local_cot = lax.dynamic_slice_in_dim(grad_out, start, SEQ_LEN, 0)
        seq_length = lax.dynamic_slice_in_dim(lengths, micro_index, 1, 0)[0]
        valid = (jnp.arange(SEQ_LEN) < seq_length)[:, None]
        forward_weights = (
            lax.all_gather(norm_gain, "dp", axis=0, tiled=True),
            lax.all_gather(w_gate, "dp", axis=0, tiled=True),
            lax.all_gather(w_value, "dp", axis=0, tiled=True),
            lax.all_gather(w_bc, "dp", axis=0, tiled=True),
            lax.all_gather(w_dt, "dp", axis=0, tiled=True),
            lax.all_gather(w_out, "dp", axis=0, tiled=True),
        )
        gain_rows, gate_rows, value_rows, shared_rows, step_rows, out_weight = forward_weights
        full_rows = lax.all_gather(local_rows, "tensor", axis=1, tiled=True)
        xfloat = full_rows.astype(jnp.float32)
        inverse_rms = lax.rsqrt(jnp.mean(xfloat * xfloat, -1, keepdims=True) + epsilon)
        gain_float = gain_rows.astype(jnp.float32)
        normed = (xfloat * inverse_rms * gain_float).astype(jnp.bfloat16)
        gate_proj = jnp.dot(normed, gate_rows, preferred_element_type=jnp.float32)
        value_proj = jnp.dot(normed, value_rows, preferred_element_type=jnp.float32)
        shared_in = jnp.dot(normed, shared_rows, preferred_element_type=jnp.float32)
        step_in = jnp.dot(normed, step_rows, preferred_element_type=jnp.float32)
        mixed_out, mixer_back = jax.vjp(
            mixer,
            gate_proj,
            value_proj,
            shared_in,
            step_in,
            conv_x,
            conv_bc,
            dt_bias,
            a_log,
            skip_d,
        )
        squares = lax.psum(jnp.sum(mixed_out * mixed_out, -1), "tensor")
        inverse_gate = lax.rsqrt(squares / inner_all + epsilon)[:, None]
        normed_out = (mixed_out * inverse_gate * gate_gain).astype(jnp.bfloat16)
        row_block = lax.all_to_all(normed_out, "tensor", split_axis=0, concat_axis=1, tiled=True)
        out_full = lax.all_gather(out_weight, "tensor", axis=1, tiled=True)
        branch_rows = lax.all_to_all(
            against(row_block, out_full).astype(jnp.bfloat16),
            "tensor",
            split_axis=1,
            concat_axis=0,
            tiled=True,
        ).astype(jnp.float32)
        out_local = (local_rows.astype(jnp.float32) + jnp.where(valid, branch_rows, 0.0)).astype(
            jnp.bfloat16
        )
        cotangent = jnp.where(valid, local_cot, jnp.zeros_like(local_cot))
        full_cot = lax.all_gather(cotangent, "tensor", axis=1, tiled=True)
        backward_weights = (
            lax.all_gather(norm_gain, "dp", axis=0, tiled=True),
            lax.all_gather(w_gate, "dp", axis=0, tiled=True),
            lax.all_gather(w_value, "dp", axis=0, tiled=True),
            lax.all_gather(w_bc, "dp", axis=0, tiled=True),
            lax.all_gather(w_dt, "dp", axis=0, tiled=True),
            lax.all_gather(w_out, "dp", axis=0, tiled=True),
        )
        gain_back, gate_back, value_back, shared_back, step_back, out_back = backward_weights
        acc_out = acc_out + over_rows(full_cot, normed_out)
        grad_normed_out = jnp.dot(full_cot, out_back, preferred_element_type=jnp.float32)
        acc_gain = acc_gain + jnp.sum(grad_normed_out * mixed_out * inverse_gate, 0)
        inner_sum = lax.psum(jnp.sum(grad_normed_out * gate_gain * mixed_out, -1), "tensor")
        grad_mixed = (
            inverse_gate * gate_gain * grad_normed_out
            - mixed_out * inverse_gate**3 * inner_sum[:, None] / inner_all
        )
        (
            grad_gate,
            grad_value,
            grad_shared,
            grad_step,
            grad_conv_value,
            grad_conv_shared,
            grad_bias,
            grad_rate,
            grad_skip,
        ) = mixer_back(grad_mixed)
        gate_low = grad_gate.astype(jnp.bfloat16)
        value_low = grad_value.astype(jnp.bfloat16)
        shared_low = grad_shared.astype(jnp.bfloat16)
        step_low = grad_step.astype(jnp.bfloat16)
        grad_normed = (
            against(gate_low, gate_back)
            + against(value_low, value_back)
            + against(shared_low, shared_back)
            + against(step_low, step_back)
        )
        acc_gate = acc_gate + over_rows(normed, gate_low)
        acc_value = acc_value + over_rows(normed, value_low)
        acc_shared = acc_shared + over_rows(normed, shared_low)
        acc_step = acc_step + over_rows(normed, step_low)
        gain_back_float = gain_back.astype(jnp.float32)
        acc_norm = acc_norm + jnp.sum(grad_normed * xfloat * inverse_rms, 0)
        grad_input = (
            inverse_rms * gain_back_float * grad_normed
            - xfloat
            * inverse_rms**3
            * jnp.sum(grad_normed * gain_back_float * xfloat, -1, keepdims=True)
            / width_all
        )
        grad_local = lax.psum_scatter(
            grad_input.astype(jnp.bfloat16), "tensor", scatter_dimension=1, tiled=True
        ).astype(jnp.float32) + cotangent.astype(jnp.float32)
        out_rows = lax.dynamic_update_slice_in_dim(out_rows, out_local, start, 0)
        grad_rows = lax.dynamic_update_slice_in_dim(grad_rows, grad_local, start, 0)
        return (
            out_rows,
            grad_rows,
            acc_gate,
            acc_value,
            acc_shared,
            acc_step,
            acc_out,
            acc_norm,
            acc_conv_value + grad_conv_value,
            acc_conv_shared + grad_conv_shared,
            acc_bias + grad_bias,
            acc_rate + grad_rate,
            acc_skip + grad_skip,
            acc_gain,
        )

    initial = (
        jnp.zeros((row_count, local_width), jnp.bfloat16),
        jnp.zeros((row_count, local_width), jnp.float32),
        jnp.zeros((width_all, inner_local), jnp.float32),
        jnp.zeros((width_all, inner_local), jnp.float32),
        jnp.zeros((width_all, w_bc.shape[1]), jnp.float32),
        jnp.zeros((width_all, w_dt.shape[1]), jnp.float32),
        jnp.zeros((width_all, inner_local), jnp.float32),
        jnp.zeros((width_all,), jnp.float32),
        jnp.zeros_like(conv_x),
        jnp.zeros_like(conv_bc),
        jnp.zeros_like(dt_bias),
        jnp.zeros_like(a_log),
        jnp.zeros_like(skip_d),
        jnp.zeros_like(gate_gain),
    )
    final = lax.fori_loop(0, micro_count, micro_step, initial)
    (
        out_rows,
        grad_rows,
        acc_gate,
        acc_value,
        acc_shared,
        acc_step,
        acc_out,
        acc_norm,
        acc_conv_value,
        acc_conv_shared,
        acc_bias,
        acc_rate,
        acc_skip,
        acc_gain,
    ) = final
    grad_gate_rows, grad_value_rows, grad_step_rows, grad_out_rows = (
        lax.psum_scatter(acc_gate, "dp", scatter_dimension=0, tiled=True),
        lax.psum_scatter(acc_value, "dp", scatter_dimension=0, tiled=True),
        lax.psum_scatter(acc_step, "dp", scatter_dimension=0, tiled=True),
        lax.psum_scatter(acc_out, "dp", scatter_dimension=0, tiled=True),
    )
    grad_shared_rows, grad_norm_rows = (
        lax.psum_scatter(acc_shared, ("dp", "tensor"), scatter_dimension=0, tiled=True),
        lax.psum_scatter(acc_norm, ("dp", "tensor"), scatter_dimension=0, tiled=True),
    )
    grad_conv_value, grad_bias, grad_rate, grad_skip, grad_gain = lax.psum(
        (acc_conv_value, acc_bias, acc_rate, acc_skip, acc_gain), "dp"
    )
    grad_conv_shared = lax.psum(acc_conv_shared, ("dp", "tensor"))
    return (
        out_rows,
        grad_rows,
        grad_norm_rows,
        grad_gate_rows,
        grad_value_rows,
        grad_shared_rows,
        grad_step_rows,
        grad_conv_value,
        grad_conv_shared,
        grad_bias,
        grad_rate,
        grad_skip,
        grad_gain,
        grad_out_rows,
    )


def solution(mesh):
    return jax.shard_map(
        per_device,
        mesh=mesh,
        in_specs=(
            P("dp", "tensor"),
            P("dp"),
            P("dp", "tensor"),
            P("dp"),
            P("dp", "tensor"),
            P("dp", "tensor"),
            P("dp", None),
            P("dp", "tensor"),
            P(None, "tensor"),
            P(),
            P("tensor"),
            P("tensor"),
            P("tensor"),
            P("tensor"),
            P("dp", "tensor"),
        ),
        out_specs=(
            P("dp", "tensor"),
            P("dp", "tensor"),
            P(("dp", "tensor")),
            P("dp", "tensor"),
            P("dp", "tensor"),
            P(("dp", "tensor"), None),
            P("dp", "tensor"),
            P(None, "tensor"),
            P(),
            P("tensor"),
            P("tensor"),
            P("tensor"),
            P("tensor"),
            P("dp", "tensor"),
        ),
        check_vma=False,
    )
```

profile of v0, /device:TPU:0, one launch (start us, length us, event | category | flops | bytes accessed | tf_op | source)
XLA Modules:
  0.0 1484.7 jit_solution(13027196084673750495)
XLA Ops:
  13.2 1059.6 %while.42 = (s32[]{:T(128)}, bf16[4096,256]{1,0:T(8,128)(2,1)}, f32[4096,256]{1,0:T(8,128)}, f32[1024,512]{1,0:T(8,128)}, f32[1024,512]{1,0:T(8,128)}, /*index=5...) while((s32[]{:T(128)}, bf16[4096,256]{1,0:T(8,128)(2,1)}, ...), condition=%wide.region_37.38_spmd.clone, body=%wide.region_0.37_spmd.clone.sunk | while | flops 44807921664 | bytes 1017131648 | solution.py:270
  22.1 22.3 %all-gather.3 = bf16[8,1,128]{2,1,0:T(2,128)(2,1)S(1)} all-gather(bf16[1,1,128]{2,1,0:T(2,128)(2,1)S(1)} %bitcast.471), channel_id=1, replica_groups=mesh['dp'=8,'tensor'=4] {'dp'}, dimensions={0}, use_global_device_ids=true | all-gather | bytes 2304 | tf_op jit(solution)/shard_map/while/body/eval_jaxpr/all_gather | solution.py:135
  44.5 26.4 %all_gather.106 = bf16[1024,8]{0,1:T(8,128)(2,1)S(1)} all-gather(bf16[128,8]{0,1:T(8,128)(2,1)S(1)} %get-tuple-element.1370), channel_id=1, replica_groups=mesh['dp'=8,'tensor'=4] {'dp'}, dimensions={0}, use_global_device_ids=true | all-gather | bytes 18432 | tf_op jit(solution)/shard_map/while/body/eval_jaxpr/all_gather | solution.py:139
  72.8 31.3 %all_gather.105 = bf16[1024,256]{1,0:T(8,128)(2,1)S(1)} all-gather(bf16[128,256]{1,0:T(8,128)(2,1)S(1)} %get-tuple-element.1373), channel_id=1, replica_groups=mesh['dp'=8,'tensor'=4] {'dp'}, dimensions={0}, use_global_device_ids=true | all-gather | bytes 589824 | tf_op jit(solution)/shard_map/while/body/eval_jaxpr/all_gather | solution.py:138
  124.1 13.0 all-gather.13.cloned.1.call-done
  176.9 20.4 %fusion.380 = f32[8,256,8,64]{1,3,2,0:T(8,128)} fusion(f32[8,8,64,256]{3,2,1,0:T(8,128)S(1)} %fusion.378, f32[8,256,8]{1,2,0:T(8,128)S(1)} %get-tuple-element.1222, f32[8,8,256]{2,1,0:T(8,128)S(1)} %get-tuple-element.1221, f32[8,256,256]{2,1,0:T(8,128)S(1)} %fusion.379, pred[256,256]{1,0:T(8,128)(4,1)S(1)} %iota_compare_fusion.7, ...), kind=kOutput, calls=%fused_computation.51.clone.1 | convolution fusion | flops 3236954112 | bytes 14942208 | tf_op jit(solution)/shard_map/while/body/eval_jaxpr/jvp(bhqs,bshp->bqhp)/dot_general | solution.py:34
  212.1 12.8 multiply_reduce_fusion.24
  247.6 13.3 multiply_reduce_fusion.26
  308.1 25.1 %fusion.381 = (f32[8,8,256]{2,1,0:T(8,128)}, f32[8,8,256]{2,1,0:T(8,128)}, f32[8,256,256]{2,1,0:T(8,128)}) fusion(f32[8,8,256]{2,1,0:T(8,128)S(1)} %get-tuple-element.1221, f32[8,256,256]{2,1,0:T(8,128)S(1)} %copy-done.27, pred[256,256]{1,0:T(8,128)(4,1)S(1)} %copy-done.40, f32[8,256,8,64]{1,3,2,0:T(8,128)S(1)} %copy-done.1, ...), kind=kOutput, calls=%fused_computation.12.clone.1 | convolution fusion | flops 3259465728 | bytes 12910592 | tf_op jit(solution)/shard_map/while/body/eval_jaxpr/transpose(jvp(bhqs,bshp->bqhp))/dot_general | solution.py:34
  344.6 20.5 %reduce-window.49 = f32[8,8,2,128]{3,1,2,0:T(8,128)S(1)} reduce-window(f32[8,8,2,128]{3,1,2,0:T(8,128)} %fusion.386, f32[]{:T(128)} %constant.161.clone.1..sunk), window={size=1x1x1x128 pad=0_0x0_0x0_0x0_127}, to_apply=%region_17.17 | reduce-window | flops 2080768 | bytes 131076 | tf_op jit(solution)/shard_map/reduce-window.18
  365.3 18.4 %multiply_reduce_fusion.29 = (f32[8,256,8]{1,2,0:T(8,128)S(1)}, f32[8,256,8,64]{1,3,2,0:T(8,128)}) fusion(f32[8,256,8,64]{1,3,2,0:T(8,128)} %copy.347, f32[8,256,8]{1,2,0:T(8,128)S(1)} %bitcast.432, f32[8,8,256]{2,1,0:T(8,128)S(1)} %get-tuple-element.1221, f32[8,256,256]{2,1,0:T(8,128)} %copy-done.26, pred[256,256]{1,0:T(8,128)(4,1)} %copy-done.39, ...), kind=kOutput, calls=%fused_computation.61.clone.1 | convolution fusion | flops 3239034880 | bytes 19202048 | tf_op jit(solution)/shard_map/while/body/eval_jaxpr/transpose(jvp(bhqs,bshp->bqhp))/dot_general | solution.py:34
  415.2 9.5 multiply_reduce_fusion.31
  449.6 10.2 fusion.397
  488.4 27.1 %all-to-all-done = bf16[4,512,512]{1,2,0:T(8,128)(2,1)} async-done(((bf16[4,512,512]{1,2,0:T(8,128)(2,1)}), bf16[4,512,512]{1,2,0:T(8,128)(2,1)}, u32[]{:S(2)}, u32[]{:S(2)}) %all-to-all-start) | async-done | bytes 2097184 | tf_op jit(solution)/shard_map/while/body/eval_jaxpr/all_to_all | solution.py:167
  554.1 16.3 %all-gather.3 = bf16[8,1,128]{2,1,0:T(2,128)(2,1)S(1)} all-gather(bf16[1,1,128]{2,1,0:T(2,128)(2,1)S(1)} %bitcast.471), channel_id=1, replica_groups=mesh['dp'=8,'tensor'=4] {'dp'}, dimensions={0}, use_global_device_ids=true | all-gather | bytes 2304 | tf_op jit(solution)/shard_map/while/body/eval_jaxpr/all_gather | solution.py:135
  570.6 26.3 %all_gather.106 = bf16[1024,8]{0,1:T(8,128)(2,1)S(1)} all-gather(bf16[128,8]{0,1:T(8,128)(2,1)S(1)} %get-tuple-element.1370), channel_id=1, replica_groups=mesh['dp'=8,'tensor'=4] {'dp'}, dimensions={0}, use_global_device_ids=true | all-gather | bytes 18432 | tf_op jit(solution)/shard_map/while/body/eval_jaxpr/all_gather | solution.py:139
  598.8 31.3 %all_gather.105 = bf16[1024,256]{1,0:T(8,128)(2,1)S(1)} all-gather(bf16[128,256]{1,0:T(8,128)(2,1)S(1)} %get-tuple-element.1373), channel_id=1, replica_groups=mesh['dp'=8,'tensor'=4] {'dp'}, dimensions={0}, use_global_device_ids=true | all-gather | bytes 589824 | tf_op jit(solution)/shard_map/while/body/eval_jaxpr/all_gather | solution.py:138
  650.0 12.5 all-gather.13.cloned.1.call-done
  702.1 20.4 %fusion.380 = f32[8,256,8,64]{1,3,2,0:T(8,128)} fusion(f32[8,8,64,256]{3,2,1,0:T(8,128)S(1)} %fusion.378, f32[8,256,8]{1,2,0:T(8,128)S(1)} %get-tuple-element.1222, f32[8,8,256]{2,1,0:T(8,128)S(1)} %get-tuple-element.1221, f32[8,256,256]{2,1,0:T(8,128)S(1)} %fusion.379, pred[256,256]{1,0:T(8,128)(4,1)S(1)} %iota_compare_fusion.7, ...), kind=kOutput, calls=%fused_computation.51.clone.1 | convolution fusion | flops 3236954112 | bytes 14942208 | tf_op jit(solution)/shard_map/while/body/eval_jaxpr/jvp(bhqs,bshp->bqhp)/dot_general | solution.py:34
  737.2 13.0 multiply_reduce_fusion.24
  772.9 13.3 multiply_reduce_fusion.26
  833.4 25.1 %fusion.381 = (f32[8,8,256]{2,1,0:T(8,128)}, f32[8,8,256]{2,1,0:T(8,128)}, f32[8,256,256]{2,1,0:T(8,128)}) fusion(f32[8,8,256]{2,1,0:T(8,128)S(1)} %get-tuple-element.1221, f32[8,256,256]{2,1,0:T(8,128)S(1)} %copy-done.27, pred[256,256]{1,0:T(8,128)(4,1)S(1)} %copy-done.40, f32[8,256,8,64]{1,3,2,0:T(8,128)S(1)} %copy-done.1, ...), kind=kOutput, calls=%fused_computation.12.clone.1 | convolution fusion | flops 3259465728 | bytes 12910592 | tf_op jit(solution)/shard_map/while/body/eval_jaxpr/transpose(jvp(bhqs,bshp->bqhp))/dot_general | solution.py:34
  869.9 20.5 %reduce-window.49 = f32[8,8,2,128]{3,1,2,0:T(8,128)S(1)} reduce-window(f32[8,8,2,128]{3,1,2,0:T(8,128)} %fusion.386, f32[]{:T(128)} %constant.161.clone.1..sunk), window={size=1x1x1x128 pad=0_0x0_0x0_0x0_127}, to_apply=%region_17.17 | reduce-window | flops 2080768 | bytes 131076 | tf_op jit(solution)/shard_map/reduce-window.18
  890.6 18.4 %multiply_reduce_fusion.29 = (f32[8,256,8]{1,2,0:T(8,128)S(1)}, f32[8,256,8,64]{1,3,2,0:T(8,128)}) fusion(f32[8,256,8,64]{1,3,2,0:T(8,128)} %copy.347, f32[8,256,8]{1,2,0:T(8,128)S(1)} %bitcast.432, f32[8,8,256]{2,1,0:T(8,128)S(1)} %get-tuple-element.1221, f32[8,256,256]{2,1,0:T(8,128)} %copy-done.26, pred[256,256]{1,0:T(8,128)(4,1)} %copy-done.39, ...), kind=kOutput, calls=%fused_computation.61.clone.1 | convolution fusion | flops 3239034880 | bytes 19202048 | tf_op jit(solution)/shard_map/while/body/eval_jaxpr/transpose(jvp(bhqs,bshp->bqhp))/dot_general | solution.py:34
  974.9 10.2 fusion.397
  1016.7 24.3 %all-to-all-done = bf16[4,512,512]{1,2,0:T(8,128)(2,1)} async-done(((bf16[4,512,512]{1,2,0:T(8,128)(2,1)}), bf16[4,512,512]{1,2,0:T(8,128)(2,1)}, u32[]{:S(2)}, u32[]{:S(2)}) %all-to-all-start) | async-done | bytes 2097184 | tf_op jit(solution)/shard_map/while/body/eval_jaxpr/all_to_all | solution.py:167
  1076.1 37.1 %all-reduce.25 = (f32[1024]{0:T(1024)S(1)}, f32[5,256]{1,0:T(8,128)}) all-reduce(f32[1024]{0:T(1024)S(1)} %copy-done.71, f32[5,256]{1,0:T(8,128)S(1)} %copy-done.59), channel_id=3, replica_groups=mesh['dp'=8,'tensor'=4] {'dp','tensor'}, use_global_device_ids=true, to_apply=%region_38.39.clone | all-reduce | flops 2304 | bytes 18432
  1113.8 37.3 %all-reduce.26 = (f32[5,512]{1,0:T(8,128)}, f32[8]{0:T(128)}, f32[8]{0:T(128)}, f32[8]{0:T(128)}, f32[512]{0:T(512)}) all-reduce(f32[5,512]{1,0:T(8,128)S(1)} %copy-done.50, f32[8]{0:T(128)S(1)} %copy-done.89, f32[8]{0:T(128)S(1)} %copy-done.92, f32[8]{0:T(128)S(1)} %copy-done.86, ...), channel_id=1, replica_groups=mesh['dp'=8,'tensor'=4] {'dp'}, use_global_device_ids=true, to_apply=%region_43.44 | all-reduce | flops 3096 | bytes 24768 | tf_op jit(solution)/shard_map/psum | solution.py:297
  1151.1 115.0 %reduce-scatter.11.cloned.1.call-done = f32[32,256]{1,0:T(8,128)} async-done(((f32[1024,256]{1,0:T(8,128)}), f32[32,256]{1,0:T(8,128)}) %reduce-scatter.11.cloned.1.call-update) | async-done | bytes 32784 | tf_op jit(solution)/shard_map/reduce_scatter | solution.py:294
  1266.1 68.2 %reduce-scatter.7.cloned.1.call-done = f32[128,512]{1,0:T(8,128)} async-done(((f32[1024,512]{1,0:T(8,128)}), f32[128,512]{1,0:T(8,128)}) %reduce-scatter.7.cloned.1.call-update) | async-done | bytes 262160 | tf_op jit(solution)/shard_map/reduce_scatter | solution.py:288
  1334.3 71.3 %reduce-scatter.9.cloned.1.call-done = f32[128,512]{1,0:T(8,128)} async-done(((f32[1024,512]{1,0:T(8,128)}), f32[128,512]{1,0:T(8,128)}) %reduce-scatter.9.cloned.1.call-update) | async-done | bytes 262160 | tf_op jit(solution)/shard_map/reduce_scatter | solution.py:289
  1405.6 71.5 %reduce-scatter.15.cloned.1.call-done = f32[128,512]{1,0:T(8,128)} async-done(((f32[1024,512]{1,0:T(8,128)}), f32[128,512]{1,0:T(8,128)}) %reduce-scatter.15.cloned.1.call-update) | async-done | bytes 262160 | tf_op jit(solution)/shard_map/reduce_scatter | solution.py:291
  (652 shorter events, 581.0 us)
Async XLA Ops:
  13.4 99.0 %copy-start.79 = (f32[1,1,8]{2,1,0:T(1,128)}, f32[1,1,8]{2,1,0:T(1,128)S(1)}, u32[]{:S(2)}) copy-start(f32[1,1,8]{2,1,0:T(1,128)S(1)} %get-tuple-element.1374) | copy-start | bytes 100 | tf_op jit(solution)/shard_map/while
  13.5 90.7 %all-gather.19.cloned.1.call-start = ((), (), s32[]{:S(2)}) async-start(), calls=%async_computation.17 | async-start | bytes 1179648 | tf_op jit(solution)/shard_map/while/body/eval_jaxpr/all_gather | solution.py:140
  14.2 90.0 %all-gather.11.cloned.1.call-start = ((), (), s32[]{:S(2)}) async-start(), calls=%async_computation.13 | async-start | bytes 5242880 | tf_op jit(solution)/shard_map/while/body/eval_jaxpr/all_gather | solution.py:143
  16.5 120.6 %all-gather.13.cloned.1.call-start = ((), (), s32[]{:S(2)}) async-start(), calls=%async_computation.14 | async-start | bytes 1179648 | tf_op jit(solution)/shard_map/while/body/eval_jaxpr/all_gather | solution.py:137
  17.3 194.8 %all-gather.15.cloned.1.call-start = ((), (), s32[]{:S(2)}) async-start(), calls=%async_computation.15 | async-start | bytes 1179648 | tf_op jit(solution)/shard_map/while/body/eval_jaxpr/all_gather | solution.py:136
  17.9 213.8 %all-gather.17.cloned.1.call-start = ((), (), s32[]{:S(2)}) async-start(), calls=%async_computation.16 | async-start | bytes 5242880 | tf_op jit(solution)/shard_map/while/body/eval_jaxpr/all_gather | solution.py:180
  22.0 493.5 %all-gather.21.cloned.1.call-start = ((), (), s32[]{:S(2)}) async-start(), calls=%async_computation.18 | async-start | bytes 5242880 | tf_op jit(solution)/shard_map/while/body/eval_jaxpr/all_gather | solution.py:168
  44.5 203.1 %copy-start.55 = (f32[512]{0:T(512)}, f32[512]{0:T(512)S(1)}, u32[]{:S(2)}) copy-start(f32[512]{0:T(512)S(1)} %mul.1764) | copy-start | bytes 6148 | tf_op jit(solution)/shard_map/while
  71.0 104.6 %copy-start.39 = (pred[256,256]{1,0:T(8,128)(4,1)}, pred[256,256]{1,0:T(8,128)(4,1)S(1)}, u32[]{:S(2)}) copy-start(pred[256,256]{1,0:T(8,128)(4,1)S(1)} %iota_compare_fusion.7) | copy-start | bytes 196612 | tf_op jit(solution)/shard_map/while
  72.8 69.2 %copy-start.51 = (f32[1,512]{1,0:T(1,128)}, f32[1,512]{1,0:T(1,128)S(1)}, u32[]{:S(2)}) copy-start(f32[1,512]{1,0:T(1,128)S(1)} %get-tuple-element.1207) | copy-start | bytes 6148 | tf_op jit(solution)/shard_map/while
  72.8 69.2 %copy-start.53 = (f32[1,512]{1,0:T(1,128)}, f32[1,512]{1,0:T(1,128)S(1)}, u32[]{:S(2)}) copy-start(f32[1,512]{1,0:T(1,128)S(1)} %get-tuple-element.1208) | copy-start | bytes 6148 | tf_op jit(solution)/shard_map/while
  104.1 438.3 %reduce-scatter.17.cloned.1.call-start = ((), (), s32[]{:S(2)}) async-start(), calls=%async_computation.19 | async-start | bytes 5242880 | tf_op jit(solution)/shard_map/while/body/eval_jaxpr/reduce_scatter | solution.py:232
  469.9 45.7 %all-to-all-start = ((bf16[4,512,512]{1,2,0:T(8,128)(2,1)}), bf16[4,512,512]{1,2,0:T(8,128)(2,1)}, u32[]{:S(2)}, u32[]{:S(2)}) async-start(bf16[4,512,512]{1,2,0:T(8,128)(2,1)} %copy.353), calls=%async_computation | async-start | bytes 4194304 | tf_op jit(solution)/shard_map/while/body/eval_jaxpr/all_to_all | solution.py:167
  521.8 18.1 %all-to-all-start.1 = ((bf16[512,4,256]{2,0,1:T(8,128)(2,1)}), bf16[512,4,256]{2,0,1:T(8,128)(2,1)S(1)}, u32[]{:S(2)}, u32[]{:S(2)}) async-start(bf16[512,4,256]{2,0,1:T(8,128)(2,1)} %bitcast.423), calls=%async_computation.1 | async-start | bytes 2097152 | tf_op jit(solution)/shard_map/while/body/eval_jaxpr/all_to_all | solution.py:169
  545.5 92.9 %copy-start.79 = (f32[1,1,8]{2,1,0:T(1,128)}, f32[1,1,8]{2,1,0:T(1,128)S(1)}, u32[]{:S(2)}) copy-start(f32[1,1,8]{2,1,0:T(1,128)S(1)} %get-tuple-element.1374) | copy-start | bytes 100 | tf_op jit(solution)/shard_map/while
  545.5 84.6 %all-gather.19.cloned.1.call-start = ((), (), s32[]{:S(2)}) async-start(), calls=%async_computation.17 | async-start | bytes 1179648 | tf_op jit(solution)/shard_map/while/body/eval_jaxpr/all_gather | solution.py:140
  546.2 84.0 %all-gather.11.cloned.1.call-start = ((), (), s32[]{:S(2)}) async-start(), calls=%async_computation.13 | async-start | bytes 5242880 | tf_op jit(solution)/shard_map/while/body/eval_jaxpr/all_gather | solution.py:143
  548.6 113.9 %all-gather.13.cloned.1.call-start = ((), (), s32[]{:S(2)}) async-start(), calls=%async_computation.14 | async-start | bytes 1179648 | tf_op jit(solution)/shard_map/while/body/eval_jaxpr/all_gather | solution.py:137
  549.2 188.1 %all-gather.15.cloned.1.call-start = ((), (), s32[]{:S(2)}) async-start(), calls=%async_computation.15 | async-start | bytes 1179648 | tf_op jit(solution)/shard_map/while/body/eval_jaxpr/all_gather | solution.py:136
  549.9 207.1 %all-gather.17.cloned.1.call-start = ((), (), s32[]{:S(2)}) async-start(), calls=%async_computation.16 | async-start | bytes 5242880 | tf_op jit(solution)/shard_map/while/body/eval_jaxpr/all_gather | solution.py:180
  554.1 486.9 %all-gather.21.cloned.1.call-start = ((), (), s32[]{:S(2)}) async-start(), calls=%async_computation.18 | async-start | bytes 5242880 | tf_op jit(solution)/shard_map/while/body/eval_jaxpr/all_gather | solution.py:168
  570.6 202.3 %copy-start.55 = (f32[512]{0:T(512)}, f32[512]{0:T(512)S(1)}, u32[]{:S(2)}) copy-start(f32[512]{0:T(512)S(1)} %mul.1764) | copy-start | bytes 6148 | tf_op jit(solution)/shard_map/while
  596.9 103.8 %copy-start.39 = (pred[256,256]{1,0:T(8,128)(4,1)}, pred[256,256]{1,0:T(8,128)(4,1)S(1)}, u32[]{:S(2)}) copy-start(pred[256,256]{1,0:T(8,128)(4,1)S(1)} %iota_compare_fusion.7) | copy-start | bytes 196612 | tf_op jit(solution)/shard_map/while
  598.8 68.5 %copy-start.51 = (f32[1,512]{1,0:T(1,128)}, f32[1,512]{1,0:T(1,128)S(1)}, u32[]{:S(2)}) copy-start(f32[1,512]{1,0:T(1,128)S(1)} %get-tuple-element.1207) | copy-start | bytes 6148 | tf_op jit(solution)/shard_map/while
  630.1 437.7 %reduce-scatter.17.cloned.1.call-start = ((), (), s32[]{:S(2)}) async-start(), calls=%async_computation.19 | async-start | bytes 5242880 | tf_op jit(solution)/shard_map/while/body/eval_jaxpr/reduce_scatter | solution.py:232
  995.2 45.8 %all-to-all-start = ((bf16[4,512,512]{1,2,0:T(8,128)(2,1)}), bf16[4,512,512]{1,2,0:T(8,128)(2,1)}, u32[]{:S(2)}, u32[]{:S(2)}) async-start(bf16[4,512,512]{1,2,0:T(8,128)(2,1)} %copy.353), calls=%async_computation | async-start | bytes 4194304 | tf_op jit(solution)/shard_map/while/body/eval_jaxpr/all_to_all | solution.py:167
  1047.3 18.1 %all-to-all-start.1 = ((bf16[512,4,256]{2,0,1:T(8,128)(2,1)}), bf16[512,4,256]{2,0,1:T(8,128)(2,1)S(1)}, u32[]{:S(2)}, u32[]{:S(2)}) async-start(bf16[512,4,256]{2,0,1:T(8,128)(2,1)} %bitcast.423), calls=%async_computation.1 | async-start | bytes 2097152 | tf_op jit(solution)/shard_map/while/body/eval_jaxpr/all_to_all | solution.py:169
  1072.8 78.3 %reduce-scatter.13.cloned.1.call-start = ((), (), s32[]{:S(2)}) async-start(), calls=%async_computation.11 | async-start | bytes 36864 | tf_op jit(solution)/shard_map/reduce_scatter | solution.py:290
  1073.4 192.7 %reduce-scatter.11.cloned.1.call-start = ((), (), s32[]{:S(2)}) async-start(), calls=%async_computation.10 | async-start | bytes 1081344 | tf_op jit(solution)/shard_map/reduce_scatter | solution.py:294
  1074.0 260.3 %reduce-scatter.7.cloned.1.call-start = ((), (), s32[]{:S(2)}) async-start(), calls=%async_computation.8 | async-start | bytes 2359296 | tf_op jit(solution)/shard_map/reduce_scatter | solution.py:288
  1074.6 331.0 %reduce-scatter.9.cloned.1.call-start = ((), (), s32[]{:S(2)}) async-start(), calls=%async_computation.9 | async-start | bytes 2359296 | tf_op jit(solution)/shard_map/reduce_scatter | solution.py:289
  1075.3 401.8 %reduce-scatter.15.cloned.1.call-start = ((), (), s32[]{:S(2)}) async-start(), calls=%async_computation.12 | async-start | bytes 2359296 | tf_op jit(solution)/shard_map/reduce_scatter | solution.py:291
  (181 other events, 2074.4 us)
Sparse Core Ops, SparseCore 0:
  16.4 42.9 all-gather.18
  61.0 33.5 all-gather.10
  96.7 40.3 all-gather.12
  139.1 38.9 all-gather.14
  179.5 33.7 all-gather.16
  214.7 34.9 all-gather.20
  466.0 58.0 reduce-scatter.16
  548.4 36.5 all-gather.18
  586.6 33.5 all-gather.10
  622.2 40.2 all-gather.12
  664.6 38.9 all-gather.14
  705.0 33.7 all-gather.16
  740.4 34.9 all-gather.20
  991.3 58.0 reduce-scatter.16
Sparse Core Ops, SparseCore 1:
  1077.0 50.9 reduce-scatter.12
  1130.7 135.4 reduce-scatter.10
  1270.1 64.1 reduce-scatter.6
  1338.4 67.1 reduce-scatter.8
  1409.7 67.3 reduce-scatter.14
where the time goes:
time: 1490 us; the launch traced here: 1480 us
  waiting for transfers between devices  426 us (29%)
  matrix products  400 us (27%)
  blocking collectives  256 us (17%)
  other arithmetic  207 us (14%)
  local copies, waits for them, and re-layouts  157 us (11%)
  starting transfers between devices  17.3 us (1%)
  between operations  16 us (1%)
    dot_general x6, matrix products, group_scan(): jnp.einsum('bhqs,bshp->bqhp', intersection[:, None] * decay_grid, weighte...  128 us
    reduce_scatter x1, waiting for transfers between devices, per_device(): lax.psum_scatter(acc_shared, ('dp', 'tensor'), scatter_dimension=0, tiled...  115 us
    another operation x16, other arithmetic  74.9 us
    reduce_scatter x1, waiting for transfers between devices, per_device(): lax.psum_scatter(acc_out, 'dp', scatter_dimension=0, tiled=True)  71.5 us
    reduce_scatter x1, waiting for transfers between devices, per_device(): lax.psum_scatter(acc_value, 'dp', scatter_dimension=0, tiled=True)  71.3 us
    reduce_scatter x1, waiting for transfers between devices, per_device(): lax.psum_scatter(acc_gate, 'dp', scatter_dimension=0, tiled=True)  68.2 us
    all_gather x2, blocking collectives, micro_step(): lax.all_gather(w_bc, 'dp', axis=0, tiled=True)  62.6 us
    reshape x8, local copies, waits for them, and re-layouts, group_scan(): values = values.reshape(blocks, GROUP, head_count, head_width)  57.2 us
  transfers between devices with their start and end apart: 23, of which 10 were waited for; matrix products, arithmetic and copies ran while one was open for 49% of the time, Pallas kernels for 0%

commit v1 on v0

--- a/solution.py
+++ b/solution.py
@@ -164,7 +164,12 @@
         squares = lax.psum(jnp.sum(mixed_out * mixed_out, -1), "tensor")
         inverse_gate = lax.rsqrt(squares / inner_all + epsilon)[:, None]
         normed_out = (mixed_out * inverse_gate * gate_gain).astype(jnp.bfloat16)
-        row_block = lax.all_to_all(normed_out, "tensor", split_axis=0, concat_axis=1, tiled=True)
+        row_block = jnp.concatenate(
+            lax.all_to_all(
+                jnp.stack(jnp.split(normed_out, lax.axis_size("tensor"), axis=0)), "tensor", 0, 0
+            ),
+            axis=1,
+        )
         out_full = lax.all_gather(out_weight, "tensor", axis=1, tiled=True)
         branch_rows = lax.all_to_all(
             against(row_block, out_full).astype(jnp.bfloat16),

time: 1490 us -> 1490 us (level)
    another operation x16 -> x18, other arithmetic: 74.9 us -> 78 us
  transfers between devices with their start and end apart: 23 -> 23, of which waited for: 10 -> 10; matrix products, arithmetic and copies ran while one was open for 49% -> 50% of each run, Pallas kernels for 0% -> 0%
where the time goes in v1:
time: 1490 us; the launch traced here: 1480 us
  waiting for transfers between devices  424 us (28%)
  matrix products  400 us (27%)
  blocking collectives  256 us (17%)
  other arithmetic  210 us (14%)
  local copies, waits for them, and re-layouts  157 us (11%)
  between operations  15.9 us (1%)
  starting transfers between devices  15.7 us (1%)
    dot_general x6, matrix products, group_scan(): jnp.einsum('bhqs,bshp->bqhp', intersection[:, None] * decay_grid, weighte...  128 us
    reduce_scatter x1, waiting for transfers between devices, per_device(): lax.psum_scatter(acc_shared, ('dp', 'tensor'), scatter_dimension=0, tiled...  115 us
    another operation x16, other arithmetic  74.8 us
    reduce_scatter x1, waiting for transfers between devices, per_device(): lax.psum_scatter(acc_value, 'dp', scatter_dimension=0, tiled=True)  71.6 us
    reduce_scatter x1, waiting for transfers between devices, per_device(): lax.psum_scatter(acc_out, 'dp', scatter_dimension=0, tiled=True)  71.2 us
    reduce_scatter x1, waiting for transfers between devices, per_device(): lax.psum_scatter(acc_gate, 'dp', scatter_dimension=0, tiled=True)  68.2 us
    all_gather x2, blocking collectives, micro_step(): lax.all_gather(w_bc, 'dp', axis=0, tiled=True)  62.5 us
    reshape x8, local copies, waits for them, and re-layouts, group_scan(): values = values.reshape(blocks, GROUP, head_count, head_width)  57.5 us
  transfers between devices with their start and end apart: 23, of which 10 were waited for; matrix products, arithmetic and copies ran while one was open for 50% of the time, Pallas kernels for 0%

profile of v1, /device:TPU:0, one launch (start us, length us, event | category | flops | bytes accessed | tf_op | source)
XLA Modules:
  0.0 1484.5 jit_solution(5973517461454493193)
XLA Ops:
  13.2 1059.2 %while.42 = (s32[]{:T(128)}, bf16[4096,256]{1,0:T(8,128)(2,1)}, f32[4096,256]{1,0:T(8,128)}, f32[1024,512]{1,0:T(8,128)}, f32[1024,512]{1,0:T(8,128)}, /*index=5...) while((s32[]{:T(128)}, bf16[4096,256]{1,0:T(8,128)(2,1)}, ...), condition=%wide.region_37.38_spmd.clone, body=%wide.region_0.37_spmd.clone.sunk | while | flops 44811067392 | bytes 1033908864 | solution.py:275
  22.0 22.3 %all-gather.3 = bf16[8,1,128]{2,1,0:T(2,128)(2,1)S(1)} all-gather(bf16[1,1,128]{2,1,0:T(2,128)(2,1)S(1)} %bitcast.480), channel_id=1, replica_groups=mesh['dp'=8,'tensor'=4] {'dp'}, dimensions={0}, use_global_device_ids=true | all-gather | bytes 2304 | tf_op jit(solution)/shard_map/while/body/eval_jaxpr/all_gather | solution.py:135
  44.4 26.4 %all_gather.106 = bf16[1024,8]{0,1:T(8,128)(2,1)S(1)} all-gather(bf16[128,8]{0,1:T(8,128)(2,1)S(1)} %get-tuple-element.1382), channel_id=1, replica_groups=mesh['dp'=8,'tensor'=4] {'dp'}, dimensions={0}, use_global_device_ids=true | all-gather | bytes 18432 | tf_op jit(solution)/shard_map/while/body/eval_jaxpr/all_gather | solution.py:139
  72.7 31.3 %all_gather.105 = bf16[1024,256]{1,0:T(8,128)(2,1)S(1)} all-gather(bf16[128,256]{1,0:T(8,128)(2,1)S(1)} %get-tuple-element.1385), channel_id=1, replica_groups=mesh['dp'=8,'tensor'=4] {'dp'}, dimensions={0}, use_global_device_ids=true | all-gather | bytes 589824 | tf_op jit(solution)/shard_map/while/body/eval_jaxpr/all_gather | solution.py:138
  124.0 13.2 all-gather.13.cloned.1.call-done
  176.9 20.4 %fusion.380 = f32[8,256,8,64]{1,3,2,0:T(8,128)} fusion(f32[8,8,64,256]{3,2,1,0:T(8,128)S(1)} %fusion.378, f32[8,256,8]{1,2,0:T(8,128)S(1)} %get-tuple-element.1230, f32[8,8,256]{2,1,0:T(8,128)S(1)} %get-tuple-element.1229, f32[8,256,256]{2,1,0:T(8,128)S(1)} %fusion.379, pred[256,256]{1,0:T(8,128)(4,1)S(1)} %iota_compare_fusion.7, ...), kind=kOutput, calls=%fused_computation.51.clone.1 | convolution fusion | flops 3236954112 | bytes 14942208 | tf_op jit(solution)/shard_map/while/body/eval_jaxpr/jvp(bhqs,bshp->bqhp)/dot_general | solution.py:34
  212.1 12.9 multiply_reduce_fusion.24
  247.7 13.3 multiply_reduce_fusion.26
  308.0 25.1 %fusion.381 = (f32[8,8,256]{2,1,0:T(8,128)}, f32[8,8,256]{2,1,0:T(8,128)}, f32[8,256,256]{2,1,0:T(8,128)}) fusion(f32[8,8,256]{2,1,0:T(8,128)S(1)} %get-tuple-element.1229, f32[8,256,256]{2,1,0:T(8,128)S(1)} %copy-done.28, pred[256,256]{1,0:T(8,128)(4,1)S(1)} %copy-done.41, f32[8,256,8,64]{1,3,2,0:T(8,128)S(1)} %copy-done.1, ...), kind=kOutput, calls=%fused_computation.12.clone.1 | convolution fusion | flops 3259465728 | bytes 12910592 | tf_op jit(solution)/shard_map/while/body/eval_jaxpr/transpose(jvp(bhqs,bshp->bqhp))/dot_general | solution.py:34
  344.5 20.5 %reduce-window.49 = f32[8,8,2,128]{3,1,2,0:T(8,128)S(1)} reduce-window(f32[8,8,2,128]{3,1,2,0:T(8,128)} %fusion.386, f32[]{:T(128)} %constant.161.clone.1..sunk), window={size=1x1x1x128 pad=0_0x0_0x0_0x0_127}, to_apply=%region_17.17 | reduce-window | flops 2080768 | bytes 131076 | tf_op jit(solution)/shard_map/reduce-window.18
  365.3 18.4 %multiply_reduce_fusion.29 = (f32[8,256,8]{1,2,0:T(8,128)S(1)}, f32[8,256,8,64]{1,3,2,0:T(8,128)}) fusion(f32[8,256,8,64]{1,3,2,0:T(8,128)} %copy.347, f32[8,256,8]{1,2,0:T(8,128)S(1)} %bitcast.440, f32[8,8,256]{2,1,0:T(8,128)S(1)} %get-tuple-element.1229, f32[8,256,256]{2,1,0:T(8,128)} %copy-done.27, pred[256,256]{1,0:T(8,128)(4,1)} %copy-done.40, ...), kind=kOutput, calls=%fused_computation.61.clone.1 | convolution fusion | flops 3239034880 | bytes 19202048 | tf_op jit(solution)/shard_map/while/body/eval_jaxpr/transpose(jvp(bhqs,bshp->bqhp))/dot_general | solution.py:34
  415.3 9.6 multiply_reduce_fusion.31
  449.8 9.8 fusion.397
  487.1 25.7 %all-to-all-done = bf16[4,512,512]{2,1,0:T(8,128)(2,1)S(1)} async-done(((bf16[4,512,512]{2,1,0:T(8,128)(2,1)}), bf16[4,512,512]{2,1,0:T(8,128)(2,1)S(1)}, u32[]{:S(2)}, u32[]{:S(2)}) %all-to-all-start) | async-done | bytes 2097184 | tf_op jit(solution)/shard_map/while/body/eval_jaxpr/all_to_all | solution.py:168
  553.8 16.3 %all-gather.3 = bf16[8,1,128]{2,1,0:T(2,128)(2,1)S(1)} all-gather(bf16[1,1,128]{2,1,0:T(2,128)(2,1)S(1)} %bitcast.480), channel_id=1, replica_groups=mesh['dp'=8,'tensor'=4] {'dp'}, dimensions={0}, use_global_device_ids=true | all-gather | bytes 2304 | tf_op jit(solution)/shard_map/while/body/eval_jaxpr/all_gather | solution.py:135
  570.2 26.4 %all_gather.106 = bf16[1024,8]{0,1:T(8,128)(2,1)S(1)} all-gather(bf16[128,8]{0,1:T(8,128)(2,1)S(1)} %get-tuple-element.1382), channel_id=1, replica_groups=mesh['dp'=8,'tensor'=4] {'dp'}, dimensions={0}, use_global_device_ids=true | all-gather | bytes 18432 | tf_op jit(solution)/shard_map/while/body/eval_jaxpr/all_gather | solution.py:139
  598.5 31.2 %all_gather.105 = bf16[1024,256]{1,0:T(8,128)(2,1)S(1)} all-gather(bf16[128,256]{1,0:T(8,128)(2,1)S(1)} %get-tuple-element.1385), channel_id=1, replica_groups=mesh['dp'=8,'tensor'=4] {'dp'}, dimensions={0}, use_global_device_ids=true | all-gather | bytes 589824 | tf_op jit(solution)/shard_map/while/body/eval_jaxpr/all_gather | solution.py:138
  649.7 12.8 all-gather.13.cloned.1.call-done
  701.8 20.4 %fusion.380 = f32[8,256,8,64]{1,3,2,0:T(8,128)} fusion(f32[8,8,64,256]{3,2,1,0:T(8,128)S(1)} %fusion.378, f32[8,256,8]{1,2,0:T(8,128)S(1)} %get-tuple-element.1230, f32[8,8,256]{2,1,0:T(8,128)S(1)} %get-tuple-element.1229, f32[8,256,256]{2,1,0:T(8,128)S(1)} %fusion.379, pred[256,256]{1,0:T(8,128)(4,1)S(1)} %iota_compare_fusion.7, ...), kind=kOutput, calls=%fused_computation.51.clone.1 | convolution fusion | flops 3236954112 | bytes 14942208 | tf_op jit(solution)/shard_map/while/body/eval_jaxpr/jvp(bhqs,bshp->bqhp)/dot_general | solution.py:34
  737.0 13.1 multiply_reduce_fusion.24
  772.7 13.3 multiply_reduce_fusion.26
  833.1 25.1 %fusion.381 = (f32[8,8,256]{2,1,0:T(8,128)}, f32[8,8,256]{2,1,0:T(8,128)}, f32[8,256,256]{2,1,0:T(8,128)}) fusion(f32[8,8,256]{2,1,0:T(8,128)S(1)} %get-tuple-element.1229, f32[8,256,256]{2,1,0:T(8,128)S(1)} %copy-done.28, pred[256,256]{1,0:T(8,128)(4,1)S(1)} %copy-done.41, f32[8,256,8,64]{1,3,2,0:T(8,128)S(1)} %copy-done.1, ...), kind=kOutput, calls=%fused_computation.12.clone.1 | convolution fusion | flops 3259465728 | bytes 12910592 | tf_op jit(solution)/shard_map/while/body/eval_jaxpr/transpose(jvp(bhqs,bshp->bqhp))/dot_general | solution.py:34
  869.6 20.5 %reduce-window.49 = f32[8,8,2,128]{3,1,2,0:T(8,128)S(1)} reduce-window(f32[8,8,2,128]{3,1,2,0:T(8,128)} %fusion.386, f32[]{:T(128)} %constant.161.clone.1..sunk), window={size=1x1x1x128 pad=0_0x0_0x0_0x0_127}, to_apply=%region_17.17 | reduce-window | flops 2080768 | bytes 131076 | tf_op jit(solution)/shard_map/reduce-window.18
  890.3 18.4 %multiply_reduce_fusion.29 = (f32[8,256,8]{1,2,0:T(8,128)S(1)}, f32[8,256,8,64]{1,3,2,0:T(8,128)}) fusion(f32[8,256,8,64]{1,3,2,0:T(8,128)} %copy.347, f32[8,256,8]{1,2,0:T(8,128)S(1)} %bitcast.440, f32[8,8,256]{2,1,0:T(8,128)S(1)} %get-tuple-element.1229, f32[8,256,256]{2,1,0:T(8,128)} %copy-done.27, pred[256,256]{1,0:T(8,128)(4,1)} %copy-done.40, ...), kind=kOutput, calls=%fused_computation.61.clone.1 | convolution fusion | flops 3239034880 | bytes 19202048 | tf_op jit(solution)/shard_map/while/body/eval_jaxpr/transpose(jvp(bhqs,bshp->bqhp))/dot_general | solution.py:34
  974.9 9.8 fusion.397
  1015.1 23.0 %all-to-all-done = bf16[4,512,512]{2,1,0:T(8,128)(2,1)S(1)} async-done(((bf16[4,512,512]{2,1,0:T(8,128)(2,1)}), bf16[4,512,512]{2,1,0:T(8,128)(2,1)S(1)}, u32[]{:S(2)}, u32[]{:S(2)}) %all-to-all-start) | async-done | bytes 2097184 | tf_op jit(solution)/shard_map/while/body/eval_jaxpr/all_to_all | solution.py:168
  1075.8 37.0 %all-reduce.25 = (f32[1024]{0:T(1024)S(1)}, f32[5,256]{1,0:T(8,128)}) all-reduce(f32[1024]{0:T(1024)S(1)} %copy-done.72, f32[5,256]{1,0:T(8,128)S(1)} %copy-done.60), channel_id=3, replica_groups=mesh['dp'=8,'tensor'=4] {'dp','tensor'}, use_global_device_ids=true, to_apply=%region_38.39.clone | all-reduce | flops 2304 | bytes 18432
  1113.4 37.4 %all-reduce.26 = (f32[5,512]{1,0:T(8,128)}, f32[8]{0:T(128)}, f32[8]{0:T(128)}, f32[8]{0:T(128)}, f32[512]{0:T(512)}) all-reduce(f32[5,512]{1,0:T(8,128)S(1)} %copy-done.51, f32[8]{0:T(128)S(1)} %copy-done.90, f32[8]{0:T(128)S(1)} %copy-done.93, f32[8]{0:T(128)S(1)} %copy-done.87, ...), channel_id=1, replica_groups=mesh['dp'=8,'tensor'=4] {'dp'}, use_global_device_ids=true, to_apply=%region_43.44 | all-reduce | flops 3096 | bytes 24768 | tf_op jit(solution)/shard_map/psum | solution.py:302
  1150.8 115.1 %reduce-scatter.11.cloned.1.call-done = f32[32,256]{1,0:T(8,128)} async-done(((f32[1024,256]{1,0:T(8,128)}), f32[32,256]{1,0:T(8,128)}) %reduce-scatter.11.cloned.1.call-update) | async-done | bytes 32784 | tf_op jit(solution)/shard_map/reduce_scatter | solution.py:299
  1265.9 68.2 %reduce-scatter.7.cloned.1.call-done = f32[128,512]{1,0:T(8,128)} async-done(((f32[1024,512]{1,0:T(8,128)}), f32[128,512]{1,0:T(8,128)}) %reduce-scatter.7.cloned.1.call-update) | async-done | bytes 262160 | tf_op jit(solution)/shard_map/reduce_scatter | solution.py:293
  1334.1 71.6 %reduce-scatter.9.cloned.1.call-done = f32[128,512]{1,0:T(8,128)} async-done(((f32[1024,512]{1,0:T(8,128)}), f32[128,512]{1,0:T(8,128)}) %reduce-scatter.9.cloned.1.call-update) | async-done | bytes 262160 | tf_op jit(solution)/shard_map/reduce_scatter | solution.py:294
  1405.7 71.2 %reduce-scatter.15.cloned.1.call-done = f32[128,512]{1,0:T(8,128)} async-done(((f32[1024,512]{1,0:T(8,128)}), f32[128,512]{1,0:T(8,128)}) %reduce-scatter.15.cloned.1.call-update) | async-done | bytes 262160 | tf_op jit(solution)/shard_map/reduce_scatter | solution.py:296
  (660 shorter events, 583.2 us)
Async XLA Ops:
  13.4 98.9 %copy-start.80 = (f32[1,1,8]{2,1,0:T(1,128)}, f32[1,1,8]{2,1,0:T(1,128)S(1)}, u32[]{:S(2)}) copy-start(f32[1,1,8]{2,1,0:T(1,128)S(1)} %get-tuple-element.1386) | copy-start | bytes 100 | tf_op jit(solution)/shard_map/while
  13.4 90.6 %all-gather.19.cloned.1.call-start = ((), (), s32[]{:S(2)}) async-start(), calls=%async_computation.17 | async-start | bytes 1179648 | tf_op jit(solution)/shard_map/while/body/eval_jaxpr/all_gather | solution.py:140
  14.1 90.0 %all-gather.11.cloned.1.call-start = ((), (), s32[]{:S(2)}) async-start(), calls=%async_computation.13 | async-start | bytes 5242880 | tf_op jit(solution)/shard_map/while/body/eval_jaxpr/all_gather | solution.py:143
  16.5 120.7 %all-gather.13.cloned.1.call-start = ((), (), s32[]{:S(2)}) async-start(), calls=%async_computation.14 | async-start | bytes 1179648 | tf_op jit(solution)/shard_map/while/body/eval_jaxpr/all_gather | solution.py:137
  17.2 194.8 %all-gather.15.cloned.1.call-start = ((), (), s32[]{:S(2)}) async-start(), calls=%async_computation.15 | async-start | bytes 1179648 | tf_op jit(solution)/shard_map/while/body/eval_jaxpr/all_gather | solution.py:136
  17.8 213.9 %all-gather.17.cloned.1.call-start = ((), (), s32[]{:S(2)}) async-start(), calls=%async_computation.16 | async-start | bytes 5242880 | tf_op jit(solution)/shard_map/while/body/eval_jaxpr/all_gather | solution.py:185
  21.9 493.2 %all-gather.21.cloned.1.call-start = ((), (), s32[]{:S(2)}) async-start(), calls=%async_computation.18 | async-start | bytes 5242880 | tf_op jit(solution)/shard_map/while/body/eval_jaxpr/all_gather | solution.py:173
  44.4 203.2 %copy-start.56 = (f32[512]{0:T(512)}, f32[512]{0:T(512)S(1)}, u32[]{:S(2)}) copy-start(f32[512]{0:T(512)S(1)} %mul.1764) | copy-start | bytes 6148 | tf_op jit(solution)/shard_map/while
  70.9 104.7 %copy-start.40 = (pred[256,256]{1,0:T(8,128)(4,1)}, pred[256,256]{1,0:T(8,128)(4,1)S(1)}, u32[]{:S(2)}) copy-start(pred[256,256]{1,0:T(8,128)(4,1)S(1)} %iota_compare_fusion.7) | copy-start | bytes 196612 | tf_op jit(solution)/shard_map/while
  72.7 69.4 %copy-start.52 = (f32[1,512]{1,0:T(1,128)}, f32[1,512]{1,0:T(1,128)S(1)}, u32[]{:S(2)}) copy-start(f32[1,512]{1,0:T(1,128)S(1)} %get-tuple-element.1215) | copy-start | bytes 6148 | tf_op jit(solution)/shard_map/while
  72.7 69.4 %copy-start.54 = (f32[1,512]{1,0:T(1,128)}, f32[1,512]{1,0:T(1,128)S(1)}, u32[]{:S(2)}) copy-start(f32[1,512]{1,0:T(1,128)S(1)} %get-tuple-element.1216) | copy-start | bytes 6148 | tf_op jit(solution)/shard_map/while
  104.0 437.8 %reduce-scatter.17.cloned.1.call-start = ((), (), s32[]{:S(2)}) async-start(), calls=%async_computation.19 | async-start | bytes 5242880 | tf_op jit(solution)/shard_map/while/body/eval_jaxpr/reduce_scatter | solution.py:237
  469.0 43.7 %all-to-all-start = ((bf16[4,512,512]{2,1,0:T(8,128)(2,1)}), bf16[4,512,512]{2,1,0:T(8,128)(2,1)S(1)}, u32[]{:S(2)}, u32[]{:S(2)}) async-start(bf16[4,512,512]{2,1,0:T(8,128)(2,1)} %pad_maximum_fusion.2), calls=%async_computation | async-start | bytes 4194304 | tf_op jit(solution)/shard_map/while/body/eval_jaxpr/all_to_all | solution.py:168
  521.5 17.9 %all-to-all-start.1 = ((bf16[512,4,256]{2,0,1:T(8,128)(2,1)}), bf16[512,4,256]{2,0,1:T(8,128)(2,1)S(1)}, u32[]{:S(2)}, u32[]{:S(2)}) async-start(bf16[512,4,256]{2,0,1:T(8,128)(2,1)} %bitcast.431), calls=%async_computation.1 | async-start | bytes 2097152 | tf_op jit(solution)/shard_map/while/body/eval_jaxpr/all_to_all | solution.py:174
  545.1 92.9 %copy-start.80 = (f32[1,1,8]{2,1,0:T(1,128)}, f32[1,1,8]{2,1,0:T(1,128)S(1)}, u32[]{:S(2)}) copy-start(f32[1,1,8]{2,1,0:T(1,128)S(1)} %get-tuple-element.1386) | copy-start | bytes 100 | tf_op jit(solution)/shard_map/while
  545.1 84.6 %all-gather.19.cloned.1.call-start = ((), (), s32[]{:S(2)}) async-start(), calls=%async_computation.17 | async-start | bytes 1179648 | tf_op jit(solution)/shard_map/while/body/eval_jaxpr/all_gather | solution.py:140
  545.9 83.9 %all-gather.11.cloned.1.call-start = ((), (), s32[]{:S(2)}) async-start(), calls=%async_computation.13 | async-start | bytes 5242880 | tf_op jit(solution)/shard_map/while/body/eval_jaxpr/all_gather | solution.py:143
  548.2 114.2 %all-gather.13.cloned.1.call-start = ((), (), s32[]{:S(2)}) async-start(), calls=%async_computation.14 | async-start | bytes 1179648 | tf_op jit(solution)/shard_map/while/body/eval_jaxpr/all_gather | solution.py:137
  548.8 188.1 %all-gather.15.cloned.1.call-start = ((), (), s32[]{:S(2)}) async-start(), calls=%async_computation.15 | async-start | bytes 1179648 | tf_op jit(solution)/shard_map/while/body/eval_jaxpr/all_gather | solution.py:136
  549.6 207.3 %all-gather.17.cloned.1.call-start = ((), (), s32[]{:S(2)}) async-start(), calls=%async_computation.16 | async-start | bytes 5242880 | tf_op jit(solution)/shard_map/while/body/eval_jaxpr/all_gather | solution.py:185
  553.7 486.8 %all-gather.21.cloned.1.call-start = ((), (), s32[]{:S(2)}) async-start(), calls=%async_computation.18 | async-start | bytes 5242880 | tf_op jit(solution)/shard_map/while/body/eval_jaxpr/all_gather | solution.py:173
  570.2 202.5 %copy-start.56 = (f32[512]{0:T(512)}, f32[512]{0:T(512)S(1)}, u32[]{:S(2)}) copy-start(f32[512]{0:T(512)S(1)} %mul.1764) | copy-start | bytes 6148 | tf_op jit(solution)/shard_map/while
  596.6 103.9 %copy-start.40 = (pred[256,256]{1,0:T(8,128)(4,1)}, pred[256,256]{1,0:T(8,128)(4,1)S(1)}, u32[]{:S(2)}) copy-start(pred[256,256]{1,0:T(8,128)(4,1)S(1)} %iota_compare_fusion.7) | copy-start | bytes 196612 | tf_op jit(solution)/shard_map/while
  598.5 68.8 %copy-start.52 = (f32[1,512]{1,0:T(1,128)}, f32[1,512]{1,0:T(1,128)S(1)}, u32[]{:S(2)}) copy-start(f32[1,512]{1,0:T(1,128)S(1)} %get-tuple-element.1215) | copy-start | bytes 6148 | tf_op jit(solution)/shard_map/while
  629.7 437.6 %reduce-scatter.17.cloned.1.call-start = ((), (), s32[]{:S(2)}) async-start(), calls=%async_computation.19 | async-start | bytes 5242880 | tf_op jit(solution)/shard_map/while/body/eval_jaxpr/reduce_scatter | solution.py:237
  994.1 44.0 %all-to-all-start = ((bf16[4,512,512]{2,1,0:T(8,128)(2,1)}), bf16[4,512,512]{2,1,0:T(8,128)(2,1)S(1)}, u32[]{:S(2)}, u32[]{:S(2)}) async-start(bf16[4,512,512]{2,1,0:T(8,128)(2,1)} %pad_maximum_fusion.2), calls=%async_computation | async-start | bytes 4194304 | tf_op jit(solution)/shard_map/while/body/eval_jaxpr/all_to_all | solution.py:168
  1046.8 18.1 %all-to-all-start.1 = ((bf16[512,4,256]{2,0,1:T(8,128)(2,1)}), bf16[512,4,256]{2,0,1:T(8,128)(2,1)S(1)}, u32[]{:S(2)}, u32[]{:S(2)}) async-start(bf16[512,4,256]{2,0,1:T(8,128)(2,1)} %bitcast.431), calls=%async_computation.1 | async-start | bytes 2097152 | tf_op jit(solution)/shard_map/while/body/eval_jaxpr/all_to_all | solution.py:174
  1072.5 78.3 %reduce-scatter.13.cloned.1.call-start = ((), (), s32[]{:S(2)}) async-start(), calls=%async_computation.11 | async-start | bytes 36864 | tf_op jit(solution)/shard_map/reduce_scatter | solution.py:295
  1073.1 192.8 %reduce-scatter.11.cloned.1.call-start = ((), (), s32[]{:S(2)}) async-start(), calls=%async_computation.10 | async-start | bytes 1081344 | tf_op jit(solution)/shard_map/reduce_scatter | solution.py:299
  1073.7 260.4 %reduce-scatter.7.cloned.1.call-start = ((), (), s32[]{:S(2)}) async-start(), calls=%async_computation.8 | async-start | bytes 2359296 | tf_op jit(solution)/shard_map/reduce_scatter | solution.py:293
  1074.2 331.5 %reduce-scatter.9.cloned.1.call-start = ((), (), s32[]{:S(2)}) async-start(), calls=%async_computation.9 | async-start | bytes 2359296 | tf_op jit(solution)/shard_map/reduce_scatter | solution.py:294
  1075.0 402.0 %reduce-scatter.15.cloned.1.call-start = ((), (), s32[]{:S(2)}) async-start(), calls=%async_computation.12 | async-start | bytes 2359296 | tf_op jit(solution)/shard_map/reduce_scatter | solution.py:296
  (183 other events, 2063.3 us)
Sparse Core Ops, SparseCore 0:
  16.3 42.9 all-gather.18
  60.9 33.7 all-gather.10
  96.8 40.3 all-gather.12
  139.2 38.9 all-gather.14
  179.6 33.7 all-gather.16
  214.8 34.9 all-gather.20
  465.8 56.6 reduce-scatter.16
  548.1 36.7 all-gather.18
  586.4 33.6 all-gather.10
  622.2 40.2 all-gather.12
  664.6 38.9 all-gather.14
  705.0 33.6 all-gather.16
  740.4 34.9 all-gather.20
  990.8 56.7 reduce-scatter.16
Sparse Core Ops, SparseCore 1:
  1076.7 51.0 reduce-scatter.12
  1130.4 135.4 reduce-scatter.10
  1269.9 64.2 reduce-scatter.6
  1338.2 67.4 reduce-scatter.8
  1409.9 67.1 reduce-scatter.14
